TPU v7x, 512 devices: a whole 4x4x16 slice. The times are simulated.
512 devices in a mesh: pair: 64 (over x, y, z_hi), sector: 8 (over z_lo, core).
Axes of the slice: x: 4, y: 4, z: 16 (z_hi: 4, z_lo: 4; z = z_hi * 4 + z_lo), core: 2. Of those that a mesh axis runs over, the one named last changes fastest.
Arguments:
- site_tensor: bfloat16 [4, 16, 128, 128], P(None, 'sector', 'pair'), may hold values from -0.5 to 0.5
- operators: bfloat16 [1536, 16, 128, 128], P('pair', 'sector'), may hold values from -6 to 6
- one_index: bfloat16 [128, 16, 128, 128], P('pair', 'sector'), may hold values from -6 to 6
- weights: bfloat16 [1536, 128], P('pair'), may hold values from -1 to 1
- comp_charge: int32 [1536], P('pair'), may hold values from 0 to 2
- one_charge: int32 [128], replicated, may hold values from 0 to 2
- sector_size: int32 [16], replicated, may hold values from 1 to 128, 1280 in all
- coupling: int32 [16, 4], replicated, may hold values from 0 to 16, as said below
Outputs:
- renormalized: bfloat16 [1536, 16, 128, 128], P('pair', 'sector')
Inputs may be any that keep to these rules, and one draw needn't show every extreme that they name: coupling[s, t] = min(s + c[t], 16) where c is an arrangement of the charges 0, 1, 1, 2 over the 4 orbital states; the value 16 marks a dropped combination.
All inputs are finite; a program needn't handle non-finite values.
Results may differ from a plain program's by a relative error of at most 0.007.
Values may be sent and summed in bfloat16 or wider, within the bound.
No kernel may reach another device: no remote copies, remote signals or barrier semaphores. Data moves between devices by JAX's collectives and lax.ppermute only.
A program may use at most 64 MiB of HBM per device.

v0:
```python
import jax
import jax.numpy as jnp
from jax import lax
from jax.sharding import PartitionSpec as P


def from_behind(value, axis, steps):
    count = lax.axis_size(axis)
    initial, last = (max(0, -steps), min(count, count - steps))
    return lax.ppermute(value, axis, [(source, source + steps) for source in range(initial, last)])


def body(
    site_tensor, operators, one_index, weights, comp_charge, one_charge, sector_size, coupling
):
    sec_local = operators.shape[1]
    block_size = operators.shape[2]
    ops_local = operators.shape[0]
    states = site_tensor.shape[0]
    total_sectors = sec_local * lax.axis_size("sector")
    first_sector = lax.axis_index("sector") * sec_local
    full_site = lax.all_gather(site_tensor, "pair", axis=2, tiled=True)
    positions = jnp.arange(block_size, dtype=jnp.int32)
    own_sizes = lax.dynamic_slice_in_dim(sector_size, first_sector, sec_local)
    live_rows = positions[None, :] < own_sizes[:, None]
    own_site = jnp.where(live_rows[None, :, :, None], full_site, jnp.zeros((), jnp.bfloat16))
    upper_blocks = from_behind(own_site, "sector", -1)
    right_pool = jnp.concatenate([own_site, upper_blocks], axis=1)
    matching = comp_charge[:, None] == one_charge[None, :]
    coef = jnp.where(matching, weights, jnp.zeros((), jnp.bfloat16))
    shard_piece = lax.all_gather(one_index, "pair", axis=0, tiled=True)
    piece_rows = shard_piece.shape[0]
    flattened = shard_piece.reshape(piece_rows, -1)
    summed = jnp.dot(coef, flattened, preferred_element_type=jnp.float32)
    combined = (operators.astype(jnp.float32) + summed.reshape(operators.shape)).astype(
        jnp.bfloat16
    )
    state_charge = coupling[0]
    pool_count = right_pool.shape[1]
    global_right = (
        first_sector + jnp.arange(sec_local, dtype=jnp.int32)[None, :] + comp_charge[:, None]
    )
    in_range = global_right < total_sectors
    pool_index = jnp.clip(global_right - first_sector, 0, pool_count - 1)
    gathered_out = jnp.zeros((ops_local, sec_local + 2, block_size, block_size), jnp.float32)
    for local_state in range(states):
        right_blocks = right_pool[local_state][pool_index]
        right_blocks = jnp.where(
            in_range[:, :, None, None], right_blocks, jnp.zeros((), jnp.bfloat16)
        )
        partial_value = jnp.einsum(
            "ksij,ksjc->ksic", combined, right_blocks, preferred_element_type=jnp.float32
        ).astype(jnp.bfloat16)
        contrib = jnp.einsum(
            "sia,ksic->ksac",
            own_site[local_state],
            partial_value,
            preferred_element_type=jnp.float32,
        )
        offset = state_charge[local_state]
        current = lax.dynamic_slice_in_dim(gathered_out, offset, sec_local, 1)
        gathered_out = lax.dynamic_update_slice_in_dim(gathered_out, current + contrib, offset, 1)
    carried = from_behind(gathered_out[:, sec_local:].astype(jnp.bfloat16), "sector", 1).astype(
        jnp.float32
    )
    landed = gathered_out[:, :sec_local].at[:, :2].add(carried)
    return landed.astype(jnp.bfloat16)


def solution(mesh):
    return jax.shard_map(
        body,
        mesh=mesh,
        in_specs=(
            P(None, "sector", "pair", None),
            P("pair", "sector", None, None),
            P("pair", "sector", None, None),
            P("pair", None),
            P("pair"),
            P(),
            P(),
            P(),
        ),
        out_specs=P("pair", "sector", None, None),
        check_vma=False,
    )
```

profile of v0, /device:TPU:38, one launch (start us, length us, event | category | flops | bytes accessed | tf_op | source)
XLA Modules:
  0.0 383.1 jit_solution(11426421221952369991)
XLA Ops:
  6.5 0.0 all-gather.2.cloned.1.call-start
  6.5 0.7 all-gather.2.cloned.1.call-update
  7.3 0.7 copy.17
  8.0 0.7 dynamic_slice.12
  8.7 249.5 %all_gather.7 = bf16[4,2,128,128]{3,0,1,2:T(4,128)(2,1)S(1)} all-gather(bf16[4,2,2,128]{3,0,1,2:T(4,128)(2,1)S(1)} %copy.17), channel_id=1, replica_groups=mesh['pair'=64,'sector'=8] {'pair'}, dimensions={2}, use_global_device_ids=true | all-gather | bytes 266240 | tf_op jit(solution)/shard_map/all_gather | solution.py:22
  258.2 0.1 iota_compare_fusion
  258.3 0.1 copy_select_fusion.16
  258.4 1.9 collective-permute-start
  260.3 0.7 compare_select_fusion
  261.1 0.1 reshape.165
  261.2 1.4 fusion.49
  270.1 0.7 add_compare_fusion
  270.9 0.0 collective-permute-done
  270.9 1.9 gather_fusion
  272.9 1.9 gather_fusion.1
  274.8 2.0 gather_fusion.2
  276.8 0.8 gather_fusion.3
  277.6 0.0 copy-start
  277.6 0.0 copy-start.1
  277.6 0.0 copy-start.2
  277.7 0.0 all-gather.2.cloned.1.call-done
  277.7 12.7 %copy.41 = bf16[128,2,128,128]{0,3,2,1:T(8,128)(2,1)} copy(bf16[128,2,128,128]{3,2,1,0:T(8,128)(2,1)} %all-gather.2.cloned.1.call-done) | data formatting | bytes 16777216 | tf_op jit(solution)/shard_map/reshape | solution.py:33
  290.4 0.0 copy-done
  290.4 0.0 copy-done.1
  290.4 0.0 copy-done.2
  290.4 8.3 %add_convert_fusion = bf16[24,2,128,128]{3,0,2,1:T(8,128)(2,1)S(1)} fusion(bf16[128,2,128,128]{0,3,2,1:T(8,128)(2,1)} %copy.41, bf16[24,2,128,128]{3,2,1,0:T(8,128)(2,1)} %param.13, bf16[24,128]{1,0:T(8,128)(2,1)S(1)} %copy-done, s32[128]{0:T(128)S(1)} %copy-done.2, s32[24]{0:T(128)S(1)} %copy-done.1), kind=kOutput, calls=%fused_computation.16 | convolution fusion | flops 203692032 | bytes 11541088 | tf_op jit(solution)/shard_map/dot_general | solution.py:34
  298.7 3.5 broadcast_in_dim.58
  302.1 4.1 %bitcast_dynamic-update-slice_fusion = f32[24,4,128,128]{2,3,0,1:T(8,128)} fusion(f32[24,4,128,128]{2,3,0,1:T(8,128)} %broadcast_in_dim.58, s32[]{:T(128)S(6)} %select_n.57, bf16[24,2,128,128]{3,2,1,0:T(8,128)(2,1)} %bitcast.73, pred[24,2]{0,1:T(4,128)(4,1)S(1)} %add_compare_fusion, bf16[24,2,128,128]{3,0,2,1:T(8,128)(2,1)S(1)} %add_convert_fusion, ...), kind=kOutput, calls=%fused_computation.15 | convolution fusion | flops 404226048 | bytes 6357508 | tf_op jit(solution)/shard_map/sia,ksic->ksac/dot_general | solution.py:54
  306.3 5.1 %fusion.5 = f32[24,4,128,128]{2,3,0,1:T(8,128)} fusion(f32[24,4,128,128]{2,3,0,1:T(8,128)} %bitcast_dynamic-update-slice_fusion, s32[]{:T(128)S(6)} %select_n.58, bf16[24,2,128,128]{3,2,1,0:T(8,128)(2,1)} %bitcast.72, pred[24,2]{0,1:T(4,128)(4,1)S(1)} %add_compare_fusion, bf16[24,2,128,128]{3,0,2,1:T(8,128)(2,1)S(1)} %add_convert_fusion, ...), kind=kOutput, calls=%fused_computation.14 | convolution fusion | flops 405012480 | bytes 9503236 | tf_op jit(solution)/shard_map/sia,ksic->ksac/dot_general | solution.py:54
  311.3 5.1 %fusion.4 = f32[24,4,128,128]{2,3,0,1:T(8,128)} fusion(f32[24,4,128,128]{2,3,0,1:T(8,128)} %fusion.5, s32[]{:T(128)S(6)} %select_n.60, bf16[24,2,128,128]{3,2,1,0:T(8,128)(2,1)} %bitcast.71, pred[24,2]{0,1:T(4,128)(4,1)S(1)} %add_compare_fusion, bf16[24,2,128,128]{3,0,2,1:T(8,128)(2,1)S(1)} %add_convert_fusion, ...), kind=kOutput, calls=%fused_computation.12 | convolution fusion | flops 405012480 | bytes 9503236 | tf_op jit(solution)/shard_map/sia,ksic->ksac/dot_general | solution.py:54
  316.4 4.6 %fusion.3 = f32[24,4,128,128]{2,3,0,1:T(8,128)} fusion(f32[24,4,128,128]{2,3,0,1:T(8,128)} %fusion.4, s32[]{:T(128)S(6)} %select_n.62, bf16[24,2,128,128]{3,2,1,0:T(8,128)(2,1)S(1)} %bitcast.70, pred[24,2]{0,1:T(4,128)(4,1)S(1)} %add_compare_fusion, bf16[24,2,128,128]{3,0,2,1:T(8,128)(2,1)S(1)} %add_convert_fusion, ...), kind=kOutput, calls=%fused_computation.10 | convolution fusion | flops 405012480 | bytes 9503236 | tf_op jit(solution)/shard_map/sia,ksic->ksac/dot_general | solution.py:54
  321.0 2.1 slice.146
  323.1 2.4 collective-permute-start.1
  325.5 46.7 %collective-permute-done.1 = bf16[24,2,128,128]{2,3,0,1:T(8,128)(2,1)S(1)} collective-permute-done((bf16[24,2,128,128]{2,3,0,1:T(8,128)(2,1)S(1)}, bf16[24,2,128,128]{2,3,0,1:T(8,128)(2,1)S(1)}, u32[]{:S(2)}, u32[]{:S(2)}) %collective-permute-start.1) | collective-permute-done | bytes 1572896 | tf_op jit(solution)/shard_map/ppermute | solution.py:10
  372.3 2.4 fusion.2
  374.7 1.6 copy.31
  (3 shorter events, 0.1 us)
Async XLA Ops:
  6.5 271.1 %all-gather.2.cloned.1.call-start = ((), (), s32[]{:S(2)}) async-start(), calls=%async_computation | async-start | bytes 8519680 | tf_op jit(solution)/shard_map/all_gather | solution.py:31
  258.4 12.5 %collective-permute-start = (bf16[4,2,128,128]{3,2,1,0:T(8,128)(2,1)S(1)}, bf16[4,2,128,128]{3,2,1,0:T(8,128)(2,1)S(1)}, u32[]{:S(2)}, u32[]{:S(2)}) collective-permute-start(bf16[4,2,128,128]{3,2,1,0:T(8,128)(2,1)S(1)} %copy_select_fusion.16), channel_id=1, source_target_pairs={{1,0},{2,1},{3,2},{4,3},{5,4},{6,5},{7,6},{9,8},{10,9},{11,10},{12... | collective-permute-start | bytes 786440 | tf_op jit(solution)/shard_map/ppermute | solution.py:10
  277.6 12.8 %copy-start = (bf16[24,128]{1,0:T(8,128)(2,1)S(1)}, bf16[24,128]{1,0:T(8,128)(2,1)}, u32[]{:S(2)}) copy-start(bf16[24,128]{1,0:T(8,128)(2,1)} %param.15) | copy-start | bytes 18436
  277.6 12.7 %copy-start.1 = (s32[24]{0:T(128)S(1)}, s32[24]{0:T(128)}, u32[]{:S(2)}) copy-start(s32[24]{0:T(128)} %param.16) | copy-start | bytes 292
  277.6 12.7 %copy-start.2 = (s32[128]{0:T(128)S(1)}, s32[128]{0:T(128)}, u32[]{:S(2)}) copy-start(s32[128]{0:T(128)} %param.17) | copy-start | bytes 1540
  323.1 49.1 %collective-permute-start.1 = (bf16[24,2,128,128]{2,3,0,1:T(8,128)(2,1)S(1)}, bf16[24,2,128,128]{2,3,0,1:T(8,128)(2,1)S(1)}, u32[]{:S(2)}, u32[]{:S(2)}) collective-permute-start(bf16[24,2,128,128]{2,3,0,1:T(8,128)(2,1)S(1)} %slice.146), channel_id=1, source_target_pairs={{0,1},{1,2},{2,3},{3,4},{4,5},{5,6},{6,7},{8,9},{9,10},{10,11},{11... | collective-permute-start | bytes 4718600 | tf_op jit(solution)/shard_map/ppermute | solution.py:10
Sparse Core Ops, SparseCore 0:
  11.5 168.6 all-gather.1
where the time goes:
time: 384 us; the launch traced here: 383 us
  blocking collectives  250 us (65%)
  waiting for transfers between devices  47.5 us (12%)
  local copies, waits for them, and re-layouts  29.5 us (8%)
  matrix products  27.1 us (7%)
  between operations  21.1 us (5%)
  starting transfers between devices  4.33 us (1%)
  other arithmetic  4.1 us (1%)
    all_gather x1, blocking collectives, body(): full_site = lax.all_gather(site_tensor, 'pair', axis=2, tiled=True)  250 us
    ppermute x2, waiting for transfers between devices, from_behind(): lax.ppermute(value, axis, [(source, source + steps) for source in range(i...  46.7 us
    dot_general x4, matrix products, body(): jnp.einsum('sia,ksic->ksac', own_site[local_state], partial_value, prefer...  18.9 us
    reshape x1, local copies, waits for them, and re-layouts, body(): flattened = shard_piece.reshape(piece_rows, -1)  12.7 us
    dot_general x1, matrix products, body(): summed = jnp.dot(coef, flattened, preferred_element_type=jnp.float32)  8.28 us
  transfers between devices with their start and end apart: 3, of which 1 were waited for; matrix products, arithmetic and copies ran while one was open for 3% of the time, Pallas kernels for 0%

commit v1 on v0

v1 whole, which is shorter than its diff:
```python
import jax
import jax.numpy as jnp
from jax import lax
from jax.experimental import pallas as pl
from jax.experimental.pallas import tpu as pltpu
from jax.sharding import Mesh, PartitionSpec as P

F32 = jnp.float32
BF16 = jnp.bfloat16
PLANE = ("x", "y")
GROUP = ("zl", "core")
VMEM = pl.BlockSpec(memory_space=pltpu.VMEM)
SMEM = pl.BlockSpec(memory_space=pltpu.SMEM)
HBM = pl.BlockSpec(memory_space=pltpu.MemorySpace.HBM)
DMA = pltpu.SemaphoreType.DMA
COEF_AT, SITE_AT, MESSAGE = 128, 160, 224


def call(body, out, ins, outs, scratch=(), flops=0, moved=4 << 20, grant=16 << 20, **more):
    return pl.pallas_call(
        body,
        out_shape=out,
        in_specs=ins,
        out_specs=outs,
        scratch_shapes=list(scratch),
        cost_estimate=pl.CostEstimate(flops=flops, bytes_accessed=moved, transcendentals=0),
        compiler_params=pltpu.CompilerParams(vmem_limit_bytes=grant),
        **more,
    )


def shift(value, steps):
    count = lax.axis_size(GROUP)
    first, last = max(0, -steps), min(count, count - steps)
    return lax.ppermute(value, GROUP, [(a, a + steps) for a in range(first, last)])


def spread_kernel(c_ref, g_ref, out_ref, sf_ref):
    planes = out_ref.shape[0]
    for half in range(2):
        for zh in range(4):
            parts = []
            for j in range(2):
                at = (j * 2 + 1 - half) * 128
                parts.append(g_ref[zh, at : at + 128, :].astype(F32).reshape(planes, 8, 128))
            to = half * 64 + zh * 16
            out_ref[:, to : to + 16, :] = jnp.concatenate(parts, axis=1).astype(BF16)
    for zh in range(4):
        piece = g_ref[zh, 512:528, :].astype(F32)
        for b in range(8):
            sf_ref[b * 8 + zh * 2 : b * 8 + zh * 2 + 2, :] = piece[2 * b : 2 * b + 2, :]
    site = sf_ref[...].astype(BF16)
    coef = c_ref[...].astype(F32)
    coef = jnp.concatenate([coef, jnp.zeros((SITE_AT - COEF_AT - c_ref.shape[0], 128), F32)], axis=0).astype(BF16)
    for d in range(planes):
        out_ref[d, COEF_AT:SITE_AT, :] = coef
        out_ref[d, SITE_AT:, :] = site


def mix(half, a_ref, out_ref, gf_ref, cf_ref):
    planes, rows = out_ref.shape[:2]
    ops = rows // 8
    coef = a_ref[:, COEF_AT : COEF_AT + ops, :].astype(F32).reshape(planes * ops, 128).astype(BF16)
    gf_ref[...] = a_ref[:, half * 64 : half * 64 + 64, :].astype(F32).reshape(1024, 128)
    for r in range(8):
        block = gf_ref[pl.ds(r, 128, stride=8), :].astype(BF16)
        cf_ref[pl.ds(r, planes * ops, stride=8), :] = jnp.dot(coef, block, preferred_element_type=F32)

    def finish(d, _):
        at = pl.multiple_of(d * rows, 16)
        out_ref[d] = cf_ref[pl.ds(at, rows), :].astype(BF16)
        return 0

    lax.fori_loop(0, planes, finish, 0, unroll=4)


def mix_one(*refs):
    mix(0, *refs)


def mix_zero(*refs):
    mix(1, *refs)


def state_order(coupling_ref):
    c = [coupling_ref[0, t] for t in range(4)]
    zero, two, low, high = (jnp.int32(0) for _ in range(4))
    for t in range(4):
        zero = jnp.where(c[t] == 0, t, zero)
        two = jnp.where(c[t] == 2, t, two)
        high = jnp.where(c[t] == 1, t, high)
    for t in reversed(range(4)):
        low = jnp.where(c[t] == 1, t, low)
    return [zero, low, high, two]


def site_kernel(coupling_ref, size_ref, a_ref, own_ref):
    first = 4 * lax.axis_index("zl") + 2 * lax.axis_index("core")
    line = lax.broadcasted_iota(jnp.int32, (128, 128), 0)
    order = state_order(coupling_ref)
    for n in range(4):
        at = pl.multiple_of(SITE_AT + order[n] * 16, 16)
        both = a_ref[:, pl.ds(at, 16), :].astype(F32)
        for s in range(2):
            block = both[:, s * 8 : (s + 1) * 8, :].reshape(128, 128)
            block = jnp.where(line < size_ref[first + s], block, 0.0)
            own_ref[s, :, n * 128 : (n + 1) * 128] = block.astype(BF16)


def combine(r_ref, own, h):
    both = r_ref[:, pl.ds(pl.multiple_of(h * 16, 16), 16), :].astype(F32)
    pair = []
    for e in range(2):
        summed = both[:, e * 8 : (e + 1) * 8, :].reshape(128, 128)
        pair.append((own[e].astype(F32) + summed).astype(BF16))
    return pair


def inner(block, right):
    return jnp.dot(block, right, preferred_element_type=F32).astype(BF16)


def joined(parts, first, last):
    return jnp.concatenate([v[:, first:last] for v in parts], axis=1)


def stacked(parts, first):
    tall = [jnp.concatenate([v[:, first : first + 128], v[:, first + 128 : first + 256]], axis=0) for v in parts]
    return jnp.concatenate(tall, axis=1)


def product(left, right):
    return jnp.dot(left, right, preferred_element_type=F32)


def pool_kernel(own_ref, up_ref, pool_ref, again_ref):
    for ref in (pool_ref, again_ref):
        for s in range(2):
            ref[s] = own_ref[s]
            ref[2 + s] = up_ref[s]


def turned(pool_ref, s, states):
    blocks = [pool_ref[s, :, n * 128 : (n + 1) * 128].astype(F32).T for n in states]
    return jnp.concatenate(blocks, axis=1).astype(BF16)


def front_kernel(charge_ref, r_ref, op_ref, pool_ref, out_ref, comb_ref, last_ref, left_ref):
    left_ref[...] = turned(pool_ref, 1, (3,))
    last_ref[:3] = pool_ref[:3, :, 384:]
    last_ref[3] = turned(pool_ref, 0, (3,))

    def step(h, _):
        pair = combine(r_ref, [op_ref[2 * h + e] for e in range(2)], h)
        parts = []
        for e in range(2):
            comb_ref[2 * h + e] = pair[e]
            parts.append(inner(pair[e], pool_ref[charge_ref[2 * h + e] + 1, :, 384:]))
        two = product(left_ref[...], joined(parts, 0, 128))
        for e in range(2):
            out_ref[2 * h + e] = two[:, e * 128 : (e + 1) * 128].astype(BF16)
        return 0

    lax.fori_loop(0, op_ref.shape[0] // 2, step, 0, unroll=4)


def middle_kernel(charge_ref, comb_ref, pool_ref, next_ref, left_ref):
    left_ref[...] = turned(pool_ref, 1, (1, 2))

    def step(h, _):
        parts = [inner(comb_ref[2 * h + e], pool_ref[charge_ref[2 * h + e] + 1, :, 128:384]) for e in range(2)]
        one = product(left_ref[...], stacked(parts, 0))
        for e in range(2):
            next_ref[2 * h + e] = one[:, e * 128 : (e + 1) * 128]
        return 0

    lax.fori_loop(0, comb_ref.shape[0] // 2, step, 0, unroll=4)


def last_kernel(charge_ref, r_ref, op_ref, next_ref, last_ref, out_ref, comb_ref):
    def step(h, _):
        pair = combine(r_ref, [op_ref[2 * h + e] for e in range(2)], h)
        parts = []
        for e in range(2):
            comb_ref[2 * h + e] = pair[e]
            parts.append(inner(pair[e], last_ref[charge_ref[2 * h + e]]))
        two = product(last_ref[3], joined(parts, 0, 128))
        for e in range(2):
            k = 2 * h + e
            out_ref[k] = (two[:, e * 128 : (e + 1) * 128] + next_ref[k]).astype(BF16)
        return 0

    lax.fori_loop(0, op_ref.shape[0] // 2, step, 0, unroll=6)


def own_kernel(charge_ref, one_ref, zero_ref, pool_ref, first_ref, second_ref, left_ref):
    left_ref[...] = jnp.concatenate([turned(pool_ref, 0, (0, 1, 2)), turned(pool_ref, 1, (0,))], axis=1)

    def step(h, _):
        low, high = [], []
        for e in range(2):
            k = 2 * h + e
            q = charge_ref[k]
            low.append(inner(zero_ref[k], pool_ref[q, :, :384]))
            high.append(inner(one_ref[k], pool_ref[q + 1, :, :128]))
        first = product(left_ref[:, :128], joined(low, 0, 128))
        second = product(left_ref[:, 128:384], stacked(low, 128)) + product(left_ref[:, 384:], joined(high, 0, 128))
        for e in range(2):
            k, at = 2 * h + e, slice(e * 128, (e + 1) * 128)
            first_ref[k] = first[:, at]
            second_ref[k] = second[:, at]
        return 0

    lax.fori_loop(0, one_ref.shape[0] // 2, step, 0, unroll=2)


def close(sector, kept_ref, came_ref, out_hbm, done_ref, sems):
    size = kept_ref.shape[0] // 3
    moves = []
    for piece in range(3):
        at = slice(piece * size, (piece + 1) * size)
        done_ref[at] = (kept_ref[at] + came_ref[at].astype(F32)).astype(BF16)
        moves.append(pltpu.make_async_copy(done_ref.at[at], out_hbm.at[at, sector], sems.at[piece]))
        moves[-1].start()
    for move in moves:
        move.wait()


def close_one(kept_ref, came_ref, out_hbm, done_ref, sems):
    close(1, kept_ref, came_ref, out_hbm, done_ref, sems)


def close_zero(kept_ref, came_ref, _, out_hbm, done_ref, sems):
    close(0, kept_ref, came_ref, out_hbm, done_ref, sems)


def body(site_tensor, operators, one_index, weights, comp_charge, one_charge, sector_size, coupling):
    ops = operators.shape[0]
    sds = jax.ShapeDtypeStruct
    column = jnp.concatenate([one_index.reshape(512, 128), site_tensor.reshape(16, 128)], axis=0)
    far = lax.all_gather(column, "zh", axis=0)
    coef = jnp.where(comp_charge[:, None] == one_charge[None, :], weights, jnp.zeros((), BF16))
    message = call(
        spread_kernel, sds((16, MESSAGE, 128), BF16), [VMEM, VMEM], VMEM, [pltpu.VMEM((64, 128), F32)]
    )(coef, far)
    near = lax.all_to_all(message, PLANE, 0, 0, tiled=True)
    rows = ops * 8
    mixed = sds((16, rows, 128), BF16)
    scratch = [pltpu.VMEM((1024, 128), F32), pltpu.VMEM((16 * rows, 128), F32)]
    flops = 2 * ops * 2 * 128**3
    half, wide, site = sds((ops, 128, 128), BF16), sds((ops, 128, 128), F32), sds((2, 128, 512), BF16)
    mixed_one = call(mix_one, mixed, [VMEM], VMEM, scratch)(near)
    landed_one = lax.all_to_all(mixed_one, PLANE, 0, 0, tiled=True)
    own = call(site_kernel, site, [SMEM, SMEM, VMEM], VMEM)(coupling, sector_size, near)
    upper = shift(own, -1)
    pool, again = call(pool_kernel, [sds((4, 128, 512), BF16)] * 2, [VMEM] * 2, [VMEM] * 2)(own, upper)
    mixed_zero = call(mix_zero, mixed, [VMEM], VMEM, scratch)(near)
    zero, one = operators[:, 0], operators[:, 1]
    landed_zero = lax.all_to_all(mixed_zero, PLANE, 0, 0, tiled=True)
    leave, comb_one, last = call(
        front_kernel,
        [half, half, sds((4, 128, 128), BF16)],
        [SMEM] + [VMEM] * 3,
        [VMEM] * 3,
        [pltpu.VMEM((128, 128), BF16)],
        flops=flops,
    )(comp_charge, landed_one, one, pool)
    came_one = shift(leave, 1)
    toward = call(
        middle_kernel, wide, [SMEM] + [VMEM] * 2, VMEM, [pltpu.VMEM((128, 256), BF16)], flops=2 * flops
    )(comp_charge, comb_one, pool)
    leave, comb_zero = call(last_kernel, [half, half], [SMEM] + [VMEM] * 4, [VMEM] * 2, flops=flops)(
        comp_charge, landed_zero, zero, toward, last
    )
    came_zero = shift(leave, 1)
    first, second = call(
        own_kernel, [wide, wide], [SMEM] + [VMEM] * 3, [VMEM] * 2, [pltpu.VMEM((128, 512), BF16)], flops=4 * flops
    )(comp_charge, comb_one, comb_zero, again)
    whole = sds((ops, 2, 128, 128), BF16)
    scratch = [pltpu.VMEM((ops, 128, 128), BF16), DMA((3,))]
    out = call(close_one, whole, [VMEM] * 2, HBM, scratch)(second, came_one)
    return call(close_zero, whole, [VMEM, VMEM, HBM], HBM, scratch, input_output_aliases={2: 0})(first, came_zero, out)


def solution(mesh):
    fine = Mesh(mesh.devices.reshape(4, 4, 4, 4, 2), ("x", "y", "zh", "zl", "core"))
    pair, sector = ("x", "y", "zh"), ("zl", "core")
    return jax.shard_map(
        body,
        mesh=fine,
        in_specs=(
            P(None, sector, pair, None),
            P(pair, sector, None, None),
            P(pair, sector, None, None),
            P(pair, None),
            P(pair),
            P(),
            P(),
            P(),
        ),
        out_specs=P(pair, sector, None, None),
        check_vma=False,
    )
```

time: 384 us -> 109 us (0.28)
  the two profiles are of different devices: /device:TPU:38 before, /device:TPU:1 now
where the time goes in v1:
time: 109 us; the launch traced here: 108 us
  blocking collectives  49 us (45%)
  starting transfers between devices  21.5 us (20%)
  Pallas kernels  19.3 us (18%)
  waiting for transfers between devices  14 us (13%)
  local copies, waits for them, and re-layouts  2.51 us (2%)
  other arithmetic  1.71 us (2%)
    all_gather x1, blocking collectives, body(): far = lax.all_gather(column, 'zh', axis=0)  31.7 us
    all_to_all x1, blocking collectives, body(): near = lax.all_to_all(message, PLANE, 0, 0, tiled=True)  17.3 us
    ppermute x3, starting transfers between devices, shift(): lax.ppermute(value, GROUP, [(a, a + steps) for a in range(first, last)])  14.2 us
    all_to_all x1, waiting for transfers between devices, body(): landed_one = lax.all_to_all(mixed_one, PLANE, 0, 0, tiled=True)  8.83 us
    ppermute x3, waiting for transfers between devices, shift(): lax.ppermute(value, GROUP, [(a, a + steps) for a in range(first, last)])  5.16 us
    pallas_call x1, Pallas kernels, body(): call(own_kernel, [wide, wide], [SMEM] + [VMEM] * 3, [VMEM] * 2, [pltpu.VM...  4.55 us
    all_to_all x1, starting transfers between devices, body(): landed_one = lax.all_to_all(mixed_one, PLANE, 0, 0, tiled=True)  3.72 us
    all_to_all x1, starting transfers between devices, body(): landed_zero = lax.all_to_all(mixed_zero, PLANE, 0, 0, tiled=True)  3.61 us
  transfers between devices with their start and end apart: 5, of which 3 were waited for; matrix products, arithmetic and copies ran while one was open for 1% of the time, Pallas kernels for 15%

profile of v1, /device:TPU:1, one launch (start us, length us, event | category | flops | bytes accessed | tf_op | source)
XLA Modules:
  0.0 108.3 jit_solution(12064854484631823414)
XLA Ops:
  0.0 0.9 pad_maximum_fusion
  0.9 31.7 %all-gather = bf16[2112,128]{1,0:T(8,128)(2,1)S(1)} all-gather(bf16[528,128]{1,0:T(8,128)(2,1)S(1)} %pad_maximum_fusion), channel_id=2, replica_groups=mesh['x'=4,'y'=4,'zh'=4,'zl'=4,'core'=2] {'zh'}, dimensions={0}, use_global_device_ids=true | all-gather | bytes 675840 | tf_op jit(solution)/shard_map/all_gather | solution.py:241
  32.6 0.8 compare_select_fusion.c_ref
  33.4 0.1 shard_map.82
  33.5 17.3 %all_to_all.15.refs_0_.a_ref = bf16[16,224,128]{2,1,0:T(8,128)(2,1)S(1)} all-to-all(bf16[16,224,128]{2,1,0:T(8,128)(2,1)S(1)} %shard_map.82), channel_id=1, replica_groups=mesh['x'=4,'y'=4,'zh'=4,'zl'=4,'core'=2] {'x','y'}, dimensions={0} | all-to-all | bytes 1835008 | tf_op jit(solution)/shard_map/all_to_all | solution.py:246
  50.9 1.5 %shard_map.83 = bf16[16,192,128]{2,1,0:T(8,128)(2,1)} custom-call(bf16[16,224,128]{2,1,0:T(8,128)(2,1)S(1)} %all_to_all.15.refs_0_.a_ref), custom_call_target="tpu_custom_call" | custom-call | bytes 4194304 | tf_op jit(solution)/shard_map/pallas_call | solution.py:252
  52.3 3.7 %all-to-all-start.1 = ((bf16[16,192,128]{2,1,0:T(8,128)(2,1)}), bf16[16,192,128]{2,1,0:T(8,128)(2,1)S(1)}, u32[]{:S(2)}, u32[]{:S(2)}) async-start(bf16[16,192,128]{2,1,0:T(8,128)(2,1)} %shard_map.83), calls=%async_computation.1 | async-start | bytes 1572864 | tf_op jit(solution)/shard_map/all_to_all | solution.py:253
  56.1 0.0 copy-start.6
  56.1 0.0 copy-start.3
  56.1 1.5 %shard_map.87 = bf16[16,192,128]{2,1,0:T(8,128)(2,1)} custom-call(bf16[16,224,128]{2,1,0:T(8,128)(2,1)S(1)} %all_to_all.15.refs_0_.a_ref), custom_call_target="tpu_custom_call" | custom-call | bytes 4194304 | tf_op jit(solution)/shard_map/pallas_call | solution.py:257
  57.6 8.8 %all-to-all-done.1.r_ref = bf16[16,192,128]{2,1,0:T(8,128)(2,1)S(1)} async-done(((bf16[16,192,128]{2,1,0:T(8,128)(2,1)}), bf16[16,192,128]{2,1,0:T(8,128)(2,1)S(1)}, u32[]{:S(2)}, u32[]{:S(2)}) %all-to-all-start.1) | async-done | bytes 786464 | tf_op jit(solution)/shard_map/all_to_all | solution.py:253
  66.4 3.6 %all-to-all-start.2 = ((bf16[16,192,128]{2,1,0:T(8,128)(2,1)}), bf16[16,192,128]{2,1,0:T(8,128)(2,1)S(1)}, u32[]{:S(2)}, u32[]{:S(2)}) async-start(bf16[16,192,128]{2,1,0:T(8,128)(2,1)} %shard_map.87), calls=%async_computation.2 | async-start | bytes 1572864 | tf_op jit(solution)/shard_map/all_to_all | solution.py:259
  70.0 0.0 copy-done.6
  70.1 0.1 copy.11.coupling_ref
  70.1 0.0 copy-done.3
  70.1 0.8 shard_map.84.own_ref
  70.9 0.0 copy-start.2
  70.9 9.2 %collective-permute-start = (bf16[2,128,512]{2,1,0:T(8,128)(2,1)S(1)}, bf16[2,128,512]{2,1,0:T(8,128)(2,1)S(1)}, u32[]{:S(2)}, u32[]{:S(2)}) collective-permute-start(bf16[2,128,512]{2,1,0:T(8,128)(2,1)S(1)} %shard_map.84.own_ref), channel_id=1, source_target_pairs={{1,0},{2,1},{3,2},{4,3},{5,4},{6,5},{7,6},{9,8},{10,9},{11,10},{12... | collective-permute-start | bytes 786440 | tf_op jit(solution)/shard_map/ppermute | solution.py:35
  80.1 1.5 %slice_bitcast_fusion = (bf16[24,128,128]{2,1,0:T(8,128)(2,1)S(1)}, bf16[24,128,128]{2,1,0:T(8,128)(2,1)S(1)}) fusion(bf16[24,2,128,128]{3,2,1,0:T(8,128)(2,1)} %param.9), kind=kLoop, calls=%fused_computation | loop fusion | bytes 3145728 | tf_op jit(solution)/shard_map/squeeze | solution.py:258
  81.6 2.9 %collective-permute-done.up_ref = bf16[2,128,512]{2,1,0:T(8,128)(2,1)S(1)} collective-permute-done((bf16[2,128,512]{2,1,0:T(8,128)(2,1)S(1)}, bf16[2,128,512]{2,1,0:T(8,128)(2,1)S(1)}, u32[]{:S(2)}, u32[]{:S(2)}) %collective-permute-start) | collective-permute-done | bytes 262176 | tf_op jit(solution)/shard_map/ppermute | solution.py:35
  84.6 0.1 shard_map.85
  84.6 0.0 copy-start.4
  84.6 0.0 copy-done.2
  84.7 2.8 %shard_map.86 = (bf16[24,128,128]{2,1,0:T(8,128)(2,1)}, bf16[24,128,128]{2,1,0:T(8,128)(2,1)S(1)}, bf16[4,128,128]{2,1,0:T(8,128)(2,1)S(1)}) custom-call(s32[24]{0:T(128)S(1)} %copy-done.2, bf16[16,192,128]{2,1,0:T(8,128)(2,1)S(1)} %all-to-all-done.1.r_ref, bf16[24,128,128]{2,1,0:T(8,128)(2,1)S(1)} %get-tuple-element.24.op_ref, ...), custom_call_target="tpu_custom_call" | custom-call | flops 201326592 | bytes 4194304 | tf_op jit(solution)/shard_map/pallas_call | solution.py:260
  87.5 1.9 %collective-permute-start.2 = (bf16[24,128,128]{2,1,0:T(8,128)(2,1)}, bf16[24,128,128]{2,1,0:T(8,128)(2,1)}, u32[]{:S(2)}, u32[]{:S(2)}) collective-permute-start(bf16[24,128,128]{2,1,0:T(8,128)(2,1)} %get-tuple-element.22), channel_id=1, source_target_pairs={{0,1},{1,2},{2,3},{3,4},{4,5},{5,6},{6,7},{8,9},{9,10},{10,11},{11... | collective-permute-start | bytes 2359304 | tf_op jit(solution)/shard_map/ppermute | solution.py:35
  89.4 0.0 copy-done.4
  89.4 3.5 %shard_map.88.next_ref = f32[24,128,128]{2,1,0:T(8,128)S(1)} custom-call(s32[24]{0:T(128)S(1)} %copy-done.2, bf16[24,128,128]{2,1,0:T(8,128)(2,1)S(1)} %get-tuple-element.15.comb_ref.one_ref, bf16[4,128,512]{2,1,0:T(8,128)(2,1)S(1)} %get-tuple-element.14.pool_ref), custom_call_target="tpu_custom_call" | custom-call | flops 402653184 | bytes 4194304 | tf_op jit(solution)/shard_map/pallas_call | solution.py:269
  92.9 0.0 copy-start
  92.9 0.9 copy-done
  93.8 0.0 all-to-all-done.2.r_ref
  93.8 0.0 copy-start.1
  93.8 0.0 copy-start.5
  93.8 1.5 %shard_map.89 = (bf16[24,128,128]{2,1,0:T(8,128)(2,1)S(1)}, bf16[24,128,128]{2,1,0:T(8,128)(2,1)S(1)}) custom-call(s32[24]{0:T(128)S(1)} %copy-done.2, bf16[16,192,128]{2,1,0:T(8,128)(2,1)S(1)} %all-to-all-done.2.r_ref, bf16[24,128,128]{2,1,0:T(8,128)(2,1)S(1)} %get-tuple-element.23.op_ref, f32[24,128,128]{2,1,0:T(8,128)S(1)} %shard_map.88.next_ref, ...), custom_call_target="tpu_custom_call" | custom-call | flops 201326592 | bytes 4194304 | tf_op jit(solution)/shard_map/pallas_call | solution.py:272
  95.3 3.1 %collective-permute-start.1 = (bf16[24,128,128]{2,1,0:T(8,128)(2,1)S(1)}, bf16[24,128,128]{2,1,0:T(8,128)(2,1)S(1)}, u32[]{:S(2)}, u32[]{:S(2)}) collective-permute-start(bf16[24,128,128]{2,1,0:T(8,128)(2,1)S(1)} %get-tuple-element.20), channel_id=1, source_target_pairs={{0,1},{1,2},{2,3},{3,4},{4,5},{5,6},{6,7},{8,9},{9,10},{10,11},{11... | collective-permute-start | bytes 2359304 | tf_op jit(solution)/shard_map/ppermute | solution.py:35
  98.4 0.0 copy-done.1
  98.4 0.0 copy-done.5
  98.5 4.6 %shard_map.90 = (f32[24,128,128]{2,1,0:T(8,128)S(1)}, f32[24,128,128]{2,1,0:T(8,128)S(1)}) custom-call(s32[24]{0:T(128)S(1)} %copy-done.2, bf16[24,128,128]{2,1,0:T(8,128)(2,1)S(1)} %copy-done.1, bf16[24,128,128]{2,1,0:T(8,128)(2,1)S(1)} %get-tuple-element.17.zero_ref, bf16[4,128,512]{2,1,0:T(8,128)(2,1)S(1)} %copy-done.5), custom_call_target="tpu_custom_call" | custom-call | flops 805306368 | bytes 4194304 | tf_op jit(solution)/shard_map/pallas_call | solution.py:276
  103.0 0.0 collective-permute-done.2.came_ref
  103.0 2.1 %shard_map.91._ = bf16[24,2,128,128]{3,2,1,0:T(8,128)(2,1)} custom-call(f32[24,128,128]{2,1,0:T(8,128)S(1)} %get-tuple-element.21.kept_ref, bf16[24,128,128]{2,1,0:T(8,128)(2,1)} %collective-permute-done.2.came_ref), custom_call_target="tpu_custom_call" | custom-call | bytes 4194304 | tf_op jit(solution)/shard_map/pallas_call | solution.py:281
  105.1 2.2 %collective-permute-done.1.came_ref = bf16[24,128,128]{2,1,0:T(8,128)(2,1)S(1)} collective-permute-done((bf16[24,128,128]{2,1,0:T(8,128)(2,1)S(1)}, bf16[24,128,128]{2,1,0:T(8,128)(2,1)S(1)}, u32[]{:S(2)}, u32[]{:S(2)}) %collective-permute-start.1) | collective-permute-done | bytes 786464 | tf_op jit(solution)/shard_map/ppermute | solution.py:35
  107.3 1.0 shard_map.92
Async XLA Ops:
  52.3 14.1 %all-to-all-start.1 = ((bf16[16,192,128]{2,1,0:T(8,128)(2,1)}), bf16[16,192,128]{2,1,0:T(8,128)(2,1)S(1)}, u32[]{:S(2)}, u32[]{:S(2)}) async-start(bf16[16,192,128]{2,1,0:T(8,128)(2,1)} %shard_map.83), calls=%async_computation.1 | async-start | bytes 1572864 | tf_op jit(solution)/shard_map/all_to_all | solution.py:253
  56.1 14.0 %copy-start.6 = (s32[16,4]{0,1:T(4,128)S(1)}, s32[16,4]{0,1:T(4,128)}, u32[]{:S(2)}) copy-start(s32[16,4]{0,1:T(4,128)} %param.15) | copy-start | bytes 772
  56.1 14.1 %copy-start.3 = (s32[16]{0:T(128)S(1)}, s32[16]{0:T(128)}, u32[]{:S(2)}) copy-start(s32[16]{0:T(128)} %size_ref.1) | copy-start | bytes 196
  66.4 27.3 %all-to-all-start.2 = ((bf16[16,192,128]{2,1,0:T(8,128)(2,1)}), bf16[16,192,128]{2,1,0:T(8,128)(2,1)S(1)}, u32[]{:S(2)}, u32[]{:S(2)}) async-start(bf16[16,192,128]{2,1,0:T(8,128)(2,1)} %shard_map.87), calls=%async_computation.2 | async-start | bytes 1572864 | tf_op jit(solution)/shard_map/all_to_all | solution.py:259
  70.9 13.7 %copy-start.2 = (s32[24]{0:T(128)S(1)}, s32[24]{0:T(128)}, u32[]{:S(2)}) copy-start(s32[24]{0:T(128)} %charge_ref.7) | copy-start | bytes 292
  70.9 13.6 %collective-permute-start = (bf16[2,128,512]{2,1,0:T(8,128)(2,1)S(1)}, bf16[2,128,512]{2,1,0:T(8,128)(2,1)S(1)}, u32[]{:S(2)}, u32[]{:S(2)}) collective-permute-start(bf16[2,128,512]{2,1,0:T(8,128)(2,1)S(1)} %shard_map.84.own_ref), channel_id=1, source_target_pairs={{1,0},{2,1},{3,2},{4,3},{5,4},{6,5},{7,6},{9,8},{10,9},{11,10},{12... | collective-permute-start | bytes 786440 | tf_op jit(solution)/shard_map/ppermute | solution.py:35
  84.6 4.8 %copy-start.4 = (bf16[4,128,512]{2,1,0:T(8,128)(2,1)}, bf16[4,128,512]{2,1,0:T(8,128)(2,1)S(1)}, u32[]{:S(2)}) copy-start(bf16[4,128,512]{2,1,0:T(8,128)(2,1)S(1)} %get-tuple-element.18.pool_ref) | copy-start | bytes 1572868
  87.5 15.5 %collective-permute-start.2 = (bf16[24,128,128]{2,1,0:T(8,128)(2,1)}, bf16[24,128,128]{2,1,0:T(8,128)(2,1)}, u32[]{:S(2)}, u32[]{:S(2)}) collective-permute-start(bf16[24,128,128]{2,1,0:T(8,128)(2,1)} %get-tuple-element.22), channel_id=1, source_target_pairs={{0,1},{1,2},{2,3},{3,4},{4,5},{5,6},{6,7},{8,9},{9,10},{10,11},{11... | collective-permute-start | bytes 2359304 | tf_op jit(solution)/shard_map/ppermute | solution.py:35
  92.9 0.9 copy-start
  93.8 4.7 %copy-start.1 = (bf16[24,128,128]{2,1,0:T(8,128)(2,1)S(1)}, bf16[24,128,128]{2,1,0:T(8,128)(2,1)}, u32[]{:S(2)}) copy-start(bf16[24,128,128]{2,1,0:T(8,128)(2,1)} %copy-done) | copy-start | bytes 2359300
  93.8 4.7 %copy-start.5 = (bf16[4,128,512]{2,1,0:T(8,128)(2,1)S(1)}, bf16[4,128,512]{2,1,0:T(8,128)(2,1)}, u32[]{:S(2)}) copy-start(bf16[4,128,512]{2,1,0:T(8,128)(2,1)} %copy-done.4) | copy-start | bytes 1572868
  95.3 12.0 %collective-permute-start.1 = (bf16[24,128,128]{2,1,0:T(8,128)(2,1)S(1)}, bf16[24,128,128]{2,1,0:T(8,128)(2,1)S(1)}, u32[]{:S(2)}, u32[]{:S(2)}) collective-permute-start(bf16[24,128,128]{2,1,0:T(8,128)(2,1)S(1)} %get-tuple-element.20), channel_id=1, source_target_pairs={{0,1},{1,2},{2,3},{3,4},{4,5},{5,6},{6,7},{8,9},{9,10},{10,11},{11... | collective-permute-start | bytes 2359304 | tf_op jit(solution)/shard_map/ppermute | solution.py:35
